TPU v7x, 128 devices: a whole 4x4x4 slice. The times are simulated.
128 devices in a mesh: phase: 4 (over z), vox: 32 (over x, y, core).
Axes of the slice: x: 4, y: 4, z: 4, core: 2. Of those that a mesh axis runs over, the one named last changes fastest.
Arguments:
- influence: float32 [4, 65536, 1536], P('phase', 'vox'), may hold values from -0.15625 to 0.15625
- weights: float32 [1536, 128], P(('phase', 'vox')), may hold values from 0.5 to 2
- warp_tiles: float32 [64, 128, 128], replicated, may hold values from -0.5 to 0.5
- owners: int32 [4, 512, 1], P('phase', 'vox'), may hold values from 0 to 31; in each aligned block of 16 rows (0 to 15, 16 to 31, ..., all dimensions but the last counted through in order) at most 2 rows name the same one
- owner_slot: int32 [4, 512], P('phase', 'vox'), may hold values from 0 to 15
- tile_index: int32 [4, 512], P('phase', 'vox'), may hold values from 0 to 63
- structure: int32 [65536], P('vox'), may hold values from 0 to 7
- prescribed: float32 [8, 128], replicated, may hold values from 0 to 3
- importance: float32 [8], replicated, may hold values from 0.25 to 4
- step_size: float32 [128], replicated, may hold values from 0.02 to 0.08
Outputs:
- new_weights: float32 [1536, 128], P(('phase', 'vox'))
- dose_field: float32 [65536, 128], P('vox')
Inputs may be any that keep to these rules, and one draw needn't show every extreme that they name: `owners`: for each phase and each device of vox, at most 2 of that device's 16 blocks name one owner, and some device reaches 2.
All inputs are finite; a program needn't handle non-finite values.
Results may differ from a plain program's by a relative error of at most 0.00023.
Values sent between devices are 32-bit elements; how exact they have to be, the bound alone decides.
A program may use at most 128 MiB of HBM per device.

v0:
```python
import jax
import jax.numpy as jnp
from jax import lax
from jax.sharding import Mesh
from jax.sharding import PartitionSpec as P

CAP = 2
NSTRUCT = 8
ITERS = 2
VOX = ("vox_0", "vox_1", "vox_2")
PHASE_VOX = ("phase", "vox_0", "vox_1", "vox_2")


def copy_for_each(shard, axis):
    copies = jnp.broadcast_to(shard, (lax.axis_size(axis), *shard.shape))
    return lax.all_to_all(copies, axis, split_axis=0, concat_axis=0, tiled=True)


def in_order(tiles, dim):
    dims = list(tiles.shape[1:])
    dims[dim] *= tiles.shape[0]
    return jnp.moveaxis(tiles, 0, dim).reshape(dims)


def gathered_by_axis(shard, axes, dim):
    far, near = axes
    first = copy_for_each(shard, far)
    tiles = jnp.swapaxes(copy_for_each(first, near), 0, 1)
    return in_order(tiles.reshape(-1, *shard.shape), dim)


def taken_together(shard, axis):
    return copy_for_each(shard, axis).sum(axis=0)


def split_up(shard, dim, length):
    before, after = (shard.shape[:dim], shard.shape[dim + 1 :])
    return jnp.moveaxis(shard.reshape(*before, length, -1, *after), dim, 0)


def sum_at_owner(shard, axis, dim):
    length = lax.axis_size(axis)
    tiles = lax.all_to_all(split_up(shard, dim, length), axis, 0, 0, tiled=True)
    return jnp.sum(tiles, axis=0)


def sum_by_axis(shard, axes, dim):
    far, near = axes
    own = sum_at_owner(split_up(shard, dim, lax.axis_size(far)), near, dim + 1)
    return jnp.sum(lax.all_to_all(own, far, 0, 0, tiled=True), axis=0)


def per_device(
    influence,
    weights,
    warp_tiles,
    owners,
    owner_slot,
    tile_index,
    structure,
    prescribed,
    importance,
    step_size,
):
    highest = lax.Precision.HIGHEST
    matrix = influence[0]
    vox_rows = matrix.shape[0]
    block_rows = warp_tiles.shape[1]
    plans = weights.shape[1]
    local_blocks = vox_rows // block_rows
    vox_count = lax.axis_size(VOX)
    slots_all = vox_count * CAP
    targets = owners[0, :, 0]
    my_slots = owner_slot[0]
    my_tiles = tile_index[0]
    positions_i = jnp.arange(local_blocks, dtype=jnp.int32)
    earlier = (targets[:, None] == targets[None, :]) & (positions_i[None, :] < positions_i[:, None])
    order_in_owner = jnp.sum(earlier.astype(jnp.int32), axis=1)
    position = targets * CAP + order_in_owner
    chosen_mask = jnp.arange(slots_all, dtype=jnp.int32)[:, None] == position[None, :]
    selector = chosen_mask.astype(jnp.float32)
    slot_sent = jnp.sum(jnp.where(chosen_mask, my_slots[None, :] + 1, 0), axis=1) - 1
    own_tiles = warp_tiles[my_tiles]
    member = (structure[:, None] == jnp.arange(NSTRUCT, dtype=jnp.int32)[None, :]).astype(
        jnp.float32
    )
    target_dose = jnp.dot(member, prescribed, precision=highest, preferred_element_type=jnp.float32)
    voxel_weight = jnp.dot(
        member, importance[:, None], precision=highest, preferred_element_type=jnp.float32
    )
    new_weights = weights
    dose_field = jnp.zeros((vox_rows, plans), jnp.float32)
    for iteration in range(ITERS):
        phase_dose = jnp.dot(
            matrix,
            gathered_by_axis(new_weights, (("phase", "vox_0", "vox_1"), "vox_2"), 0),
            precision=highest,
            preferred_element_type=jnp.float32,
        )
        blocks = phase_dose.reshape(local_blocks, block_rows, plans)
        warped = jnp.einsum("kab,kbp->kap", own_tiles, blocks, precision=highest)
        outgoing = jnp.dot(
            selector,
            warped.reshape(local_blocks, block_rows * plans),
            precision=highest,
            preferred_element_type=jnp.float32,
        )
        outgoing = outgoing.reshape(vox_count, CAP, block_rows * plans)
        labels_out = slot_sent.reshape(vox_count, CAP, 1)
        incoming, info = (
            lax.all_to_all(outgoing, VOX, split_axis=0, concat_axis=0, tiled=True),
            lax.all_to_all(labels_out, VOX, split_axis=0, concat_axis=0, tiled=True),
        )
        received_slot = info.reshape(slots_all)
        warped_in = incoming.reshape(slots_all, block_rows, plans)
        placing = (
            jnp.arange(local_blocks, dtype=jnp.int32)[:, None] == received_slot[None, :]
        ).astype(jnp.float32)
        partial_dose = jnp.dot(
            placing,
            warped_in.reshape(slots_all, block_rows * plans),
            precision=highest,
            preferred_element_type=jnp.float32,
        )
        partial_dose = partial_dose.reshape(vox_rows, plans)
        dose_field = taken_together(partial_dose, "phase")
        adjoint = voxel_weight * (dose_field - target_dose)
        adjoint_rows = adjoint.reshape(local_blocks, block_rows * plans)
        back_slots = jnp.dot(
            placing.T, adjoint_rows, precision=highest, preferred_element_type=jnp.float32
        )
        returned = lax.all_to_all(
            back_slots.reshape(vox_count, CAP, block_rows * plans),
            VOX,
            split_axis=0,
            concat_axis=0,
            tiled=True,
        )
        pulled = jnp.dot(
            selector.T,
            returned.reshape(slots_all, block_rows * plans),
            precision=highest,
            preferred_element_type=jnp.float32,
        )
        local_adjoint = jnp.einsum(
            "kab,kap->kbp",
            own_tiles,
            pulled.reshape(local_blocks, block_rows, plans),
            precision=highest,
        )
        phase_adjoint = local_adjoint.reshape(vox_rows, plans)
        gradient = sum_by_axis(
            lax.dot_general(
                matrix,
                phase_adjoint,
                (((0,), (0,)), ((), ())),
                precision=highest,
                preferred_element_type=jnp.float32,
            ),
            (("phase", "vox_0", "vox_1"), "vox_2"),
            0,
        )
        new_weights = jnp.maximum(new_weights - step_size[None, :] * gradient, 0.0)
    return (new_weights, dose_field)


def solution(mesh):
    split = Mesh(
        mesh.devices.reshape(mesh.shape["phase"], 4, 4, 2), ("phase", "vox_0", "vox_1", "vox_2")
    )
    placed = (
        P("phase", VOX, None),
        P(PHASE_VOX, None),
        P(),
        P("phase", VOX, None),
        P("phase", VOX),
        P("phase", VOX),
        P(VOX),
        P(),
        P(),
        P(),
    )
    return jax.shard_map(
        per_device,
        mesh=split,
        in_specs=placed,
        out_specs=(P(PHASE_VOX, None), P(VOX, None)),
        check_vma=False,
    )
```

profile of v0, /device:TPU:1, one launch (start us, length us, event | category | flops | bytes accessed | tf_op | source)
XLA Modules:
  0.0 584.3 jit_solution(6697933440601813835)
XLA Ops:
  0.6 1.5 broadcast_in_dim.47
  2.2 12.0 %all-to-all-start.1 = ((f32[64,12,128]{2,1,0:T(8,128)}), f32[64,12,128]{2,1,0:T(8,128)S(1)}, u32[]{:S(2)}, u32[]{:S(2)}) async-start(f32[64,12,128]{2,1,0:T(8,128)} %broadcast_in_dim.47), calls=%async_computation.1 | async-start | bytes 1048576 | tf_op jit(solution)/shard_map/all_to_all | solution.py:16
  17.8 2.8 gather_fusion
  20.7 5.4 all-to-all-done.1
  26.3 6.3 %all_to_all.76 = f32[2,64,12,128]{3,1,2,0:T(8,128)S(1)} all-to-all(f32[2,64,12,128]{3,1,2,0:T(8,128)S(1)} %broadcast_in_dim.48), channel_id=1, replica_groups=mesh['phase'=4,'vox_0'=4,'vox_1'=4,'vox_2'=2] {'vox_2'}, dimensions={0} | all-to-all | bytes 1572864 | tf_op jit(solution)/shard_map/all_to_all | solution.py:16
  32.6 3.9 all-to-all-start
  37.0 13.2 %fusion.49 = f32[16,128,128]{2,1,0:T(8,128)S(1)} fusion(f32[16,128,1536]{2,1,0:T(8,128)} %bitcast.81, f32[1536,128,1]{1,0,2:T(8,128)S(1)} %reshape.195), kind=kOutput, calls=%fused_computation.59 | convolution fusion | flops 4831838208 | bytes 14417920 | tf_op jit(solution)/shard_map/dot_general | solution.py:94
  51.6 1.9 fusion.31
  53.5 5.2 copy.113
  58.7 7.5 %all-to-all-start.3 = ((f32[32,2,16384]{2,1,0:T(2,128)}), f32[32,2,16384]{2,1,0:T(2,128)}, u32[]{:S(2)}, u32[]{:S(2)}) async-start(f32[32,2,16384]{2,1,0:T(2,128)} %copy.113), calls=%async_computation.3 | async-start | bytes 8388608 | tf_op jit(solution)/shard_map/all_to_all | solution.py:111
  67.6 50.8 %all-to-all-done.3 = f32[32,2,16384]{2,1,0:T(2,128)} async-done(((f32[32,2,16384]{2,1,0:T(2,128)}), f32[32,2,16384]{2,1,0:T(2,128)}, u32[]{:S(2)}, u32[]{:S(2)}) %all-to-all-start.3) | async-done | bytes 4194336 | tf_op jit(solution)/shard_map/all_to_all | solution.py:111
  118.4 6.0 %reshape_reshape.19 = f32[64,16384]{1,0:T(8,128)} reshape(f32[32,2,16384]{2,1,0:T(2,128)} %all-to-all-done.3) | data formatting | bytes 8388608 | tf_op jit(solution)/shard_map/reshape;reshape | solution.py:121
  124.4 3.7 fusion.36
  128.3 2.2 broadcast_in_dim.49
  130.5 5.5 all-to-all-start.4
  137.0 47.3 %all-to-all-done.4 = f32[4,2048,128]{2,1,0:T(8,128)} async-done(((f32[4,2048,128]{2,1,0:T(8,128)}), f32[4,2048,128]{2,1,0:T(8,128)}, u32[]{:S(2)}, u32[]{:S(2)}) %all-to-all-start.4) | async-done | bytes 4194336 | tf_op jit(solution)/shard_map/all_to_all | solution.py:16
  184.4 3.5 reduce_sum.74
  187.8 2.0 subtract_multiply_fusion.1
  191.0 3.1 fusion.51
  194.1 3.2 copy.115
  197.3 58.3 %all_to_all.77 = f32[32,2,16384]{2,1,0:T(2,128)} all-to-all(f32[32,2,16384]{2,1,0:T(2,128)S(1)} %copy.115), channel_id=1, replica_groups=mesh['phase'=4,'vox_0'=4,'vox_1'=4,'vox_2'=2] {'vox_0','vox_1','vox_2'}, dimensions={0} | all-to-all | bytes 8388608 | tf_op jit(solution)/shard_map/all_to_all | solution.py:132
  255.6 6.0 %reshape.177 = f32[64,16384]{1,0:T(8,128)} reshape(f32[32,2,16384]{2,1,0:T(2,128)} %all_to_all.77) | data formatting | bytes 8388608 | tf_op jit(solution)/shard_map/reshape | solution.py:141
  261.7 3.6 fusion.9
  265.3 2.2 fusion.23
  267.5 10.1 %fusion.12 = f32[1536,128]{0,1:T(8,128)S(1)} fusion(f32[2048,128]{1,0:T(8,128)S(1)} %bitcast.83, f32[1,2048,1536]{2,1,0:T(8,128)} %param.10), kind=kOutput, calls=%fused_computation.13 | convolution fusion | flops 4831838208 | bytes 14417920 | tf_op jit(solution)/shard_map/dot_general | solution.py:153
  280.5 4.1 all_to_all.78
  284.9 17.0 %all_to_all.79 = f32[64,12,128]{2,1,0:T(8,128)S(1)} all-to-all(f32[64,12,128]{2,1,0:T(8,128)S(1)} %copy.121), channel_id=1, replica_groups=mesh['phase'=4,'vox_0'=4,'vox_1'=4,'vox_2'=2] {'phase','vox_0','vox_1'}, dimensions={0} | all-to-all | bytes 786432 | tf_op jit(solution)/shard_map/all_to_all | solution.py:50
  302.1 15.4 %all_to_all.80 = f32[64,12,128]{2,1,0:T(8,128)S(1)} all-to-all(f32[64,12,128]{2,1,0:T(8,128)S(1)} %broadcast_in_dim.50), channel_id=1, replica_groups=mesh['phase'=4,'vox_0'=4,'vox_1'=4,'vox_2'=2] {'phase','vox_0','vox_1'}, dimensions={0} | all-to-all | bytes 786432 | tf_op jit(solution)/shard_map/all_to_all | solution.py:16
  317.7 7.5 %all_to_all.81 = f32[2,64,12,128]{3,1,2,0:T(8,128)S(1)} all-to-all(f32[2,64,12,128]{3,1,2,0:T(8,128)S(1)} %broadcast_in_dim.51), channel_id=1, replica_groups=mesh['phase'=4,'vox_0'=4,'vox_1'=4,'vox_2'=2] {'vox_2'}, dimensions={0} | all-to-all | bytes 1572864 | tf_op jit(solution)/shard_map/all_to_all | solution.py:16
  326.6 16.3 %fusion.15 = f32[2048,128]{0,1:T(8,128)S(1)} fusion(f32[1536,128]{1,0:T(8,128)} %reshape_reshape.21, f32[1,2048,1536]{2,1,0:T(8,128)} %param.10), kind=kOutput, calls=%fused_computation.14 | convolution fusion | flops 4831838208 | bytes 14417920 | tf_op jit(solution)/shard_map/dot_general | solution.py:94
  344.2 2.4 fusion.52
  347.7 3.1 fusion.29
  350.9 3.2 copy.125
  354.1 54.4 %all_to_all.82 = f32[32,2,16384]{2,1,0:T(2,128)} all-to-all(f32[32,2,16384]{2,1,0:T(2,128)S(1)} %copy.125), channel_id=1, replica_groups=mesh['phase'=4,'vox_0'=4,'vox_1'=4,'vox_2'=2] {'vox_0','vox_1','vox_2'}, dimensions={0} | all-to-all | bytes 8388608 | tf_op jit(solution)/shard_map/all_to_all | solution.py:111
  408.5 6.0 %reshape_reshape.22 = f32[64,16384]{1,0:T(8,128)} reshape(f32[32,2,16384]{2,1,0:T(2,128)} %all_to_all.82) | data formatting | bytes 8388608 | tf_op jit(solution)/shard_map/reshape;reshape | solution.py:121
  414.6 4.6 fusion.35
  420.9 52.4 %all_to_all.83 = f32[4,2048,128]{2,1,0:T(8,128)} all-to-all(f32[4,2048,128]{2,1,0:T(8,128)S(1)} %broadcast_in_dim.52), channel_id=1, replica_groups=mesh['phase'=4,'vox_0'=4,'vox_1'=4,'vox_2'=2] {'phase'}, dimensions={0} | all-to-all | bytes 8388608 | tf_op jit(solution)/shard_map/all_to_all | solution.py:16
  473.2 3.5 reduce_sum.77
  476.7 1.6 subtract_multiply_fusion
  478.5 1.8 fusion.53
  480.4 3.2 copy.127
  483.6 55.5 %all_to_all.84 = f32[32,2,16384]{2,1,0:T(2,128)} all-to-all(f32[32,2,16384]{2,1,0:T(2,128)S(1)} %copy.127), channel_id=1, replica_groups=mesh['phase'=4,'vox_0'=4,'vox_1'=4,'vox_2'=2] {'vox_0','vox_1','vox_2'}, dimensions={0} | all-to-all | bytes 8388608 | tf_op jit(solution)/shard_map/all_to_all | solution.py:132
  539.1 6.0 %reshape.183 = f32[64,16384]{1,0:T(8,128)} reshape(f32[32,2,16384]{2,1,0:T(2,128)} %all_to_all.84) | data formatting | bytes 8388608 | tf_op jit(solution)/shard_map/reshape | solution.py:141
  545.2 3.6 fusion.6
  548.8 2.2 fusion.21
  551.0 10.1 %fusion.18 = f32[1536,128]{0,1:T(8,128)S(1)} fusion(f32[2048,128]{1,0:T(8,128)S(1)} %bitcast.82, f32[1,2048,1536]{2,1,0:T(8,128)} %param.10), kind=kOutput, calls=%fused_computation.15 | convolution fusion | flops 4831838208 | bytes 14417920 | tf_op jit(solution)/shard_map/dot_general | solution.py:153
  562.0 4.1 all_to_all.85
  566.4 17.0 %all_to_all.86 = f32[64,12,128]{2,1,0:T(8,128)S(1)} all-to-all(f32[64,12,128]{2,1,0:T(8,128)S(1)} %copy.133), channel_id=1, replica_groups=mesh['phase'=4,'vox_0'=4,'vox_1'=4,'vox_2'=2] {'phase','vox_0','vox_1'}, dimensions={0} | all-to-all | bytes 786432 | tf_op jit(solution)/shard_map/all_to_all | solution.py:50
  (61 shorter events, 20.3 us)
Async XLA Ops:
  0.6 187.2 %copy-start = (f32[8,128]{1,0:T(8,128)S(1)}, f32[8,128]{1,0:T(8,128)}, u32[]{:S(2)}) copy-start(f32[8,128]{1,0:T(8,128)} %param.17) | copy-start | bytes 12292
  2.2 23.9 %all-to-all-start.1 = ((f32[64,12,128]{2,1,0:T(8,128)}), f32[64,12,128]{2,1,0:T(8,128)S(1)}, u32[]{:S(2)}, u32[]{:S(2)}) async-start(f32[64,12,128]{2,1,0:T(8,128)} %broadcast_in_dim.47), calls=%async_computation.1 | async-start | bytes 1048576 | tf_op jit(solution)/shard_map/all_to_all | solution.py:16
  32.6 26.1 %all-to-all-start = ((s32[32,2,1]{1,2,0:T(1,128)}), s32[32,2,1]{1,2,0:T(1,128)S(1)}, u32[]{:S(2)}, u32[]{:S(2)}) async-start(s32[32,2,1]{1,2,0:T(1,128)} %bitcast.5), calls=%async_computation | async-start | bytes 32768 | tf_op jit(solution)/shard_map/all_to_all | solution.py:112
  58.7 59.7 %all-to-all-start.3 = ((f32[32,2,16384]{2,1,0:T(2,128)}), f32[32,2,16384]{2,1,0:T(2,128)}, u32[]{:S(2)}, u32[]{:S(2)}) async-start(f32[32,2,16384]{2,1,0:T(2,128)} %copy.113), calls=%async_computation.3 | async-start | bytes 8388608 | tf_op jit(solution)/shard_map/all_to_all | solution.py:111
  130.5 5.5 copy-start.3
  130.5 5.5 copy-start.5
  130.5 53.8 %all-to-all-start.4 = ((f32[4,2048,128]{2,1,0:T(8,128)}), f32[4,2048,128]{2,1,0:T(8,128)}, u32[]{:S(2)}, u32[]{:S(2)}) async-start(f32[4,2048,128]{2,1,0:T(8,128)} %broadcast_in_dim.49), calls=%async_computation.4 | async-start | bytes 8388608 | tf_op jit(solution)/shard_map/all_to_all | solution.py:16
  278.8 23.2 %copy-start.2 = (f32[12,128]{1,0:T(8,128)S(1)}, f32[12,128]{1,0:T(8,128)}, u32[]{:S(2)}) copy-start(f32[12,128]{1,0:T(8,128)} %param.11) | copy-start | bytes 18436
  278.8 23.2 %copy-start.4 = (f32[128]{0:T(128)S(1)}, f32[128]{0:T(128)}, u32[]{:S(2)}) copy-start(f32[128]{0:T(128)} %param.19) | copy-start | bytes 1540
  561.2 22.9 %copy-start.1 = (f32[8,128]{1,0:T(8,128)S(1)}, f32[8,128]{1,0:T(8,128)}, u32[]{:S(2)}) copy-start(f32[8,128]{1,0:T(8,128)} %param.17) | copy-start | bytes 12292
where the time goes:
time: 592 us; the launch traced here: 584 us
  blocking collectives  292 us (49%)
  waiting for transfers between devices  104 us (18%)
  matrix products  85.8 us (14%)
  local copies, waits for them, and re-layouts  59.5 us (10%)
  starting transfers between devices  28.9 us (5%)
  other arithmetic  13.2 us (2%)
    all_to_all x2, blocking collectives, per_device(): lax.all_to_all(back_slots.reshape(vox_count, CAP, block_rows * plans), VO...  114 us
    all_to_all x4, blocking collectives, copy_for_each(): return lax.all_to_all(copies, axis, split_axis=0, concat_axis=0, tiled=True)  81.5 us
    all_to_all x1, blocking collectives, per_device(): lax.all_to_all(outgoing, VOX, split_axis=0, concat_axis=0, tiled=True)  54.4 us
    all_to_all x2, waiting for transfers between devices, copy_for_each(): return lax.all_to_all(copies, axis, split_axis=0, concat_axis=0, tiled=True)  52.8 us
    all_to_all x1, waiting for transfers between devices, per_device(): lax.all_to_all(outgoing, VOX, split_axis=0, concat_axis=0, tiled=True)  50.8 us
    all_to_all x2, blocking collectives, sum_by_axis(): return jnp.sum(lax.all_to_all(own, far, 0, 0, tiled=True), axis=0)  33.9 us
    dot_general x2, matrix products, per_device(): jnp.dot(matrix, gathered_by_axis(new_weights, (('phase', 'vox_0', 'vox_1'...  29.5 us
    dot_general x2, matrix products, per_device(): lax.dot_general(matrix, phase_adjoint, (((0,), (0,)), ((), ())), precisio...  20.3 us
  transfers between devices with their start and end apart: 4, of which 3 were waited for; matrix products, arithmetic and copies ran while one was open for 5% of the time, Pallas kernels for 0%

commit v1 on v0

v1 whole, which is shorter than its diff:
```python
import jax
import jax.numpy as jnp
from jax import lax
from jax.experimental import pallas as pl
from jax.experimental.pallas import tpu as pltpu
from jax.sharding import Mesh
from jax.sharding import PartitionSpec as P

AXES = ("z", "x", "y", "c")
VOX = ("x", "y", "c")
SIZES = (4, 4, 4, 2)
NDEV = 128
NVOX = 32
NSTRUCT = 8
ITERS = 2
PLANS = 128
BLK = 128
BLOCKS = 16
CHUNKS = 2
PER = BLOCKS // CHUNKS
SPOTS = 1536
OWN = SPOTS // NDEV
ROWS = BLOCKS * BLK
TARGETS = NVOX * BLOCKS
SOURCES = NDEV * BLOCKS
NTILE = 64
LOAD = 256
GROUP = 512
LOGICAL = pl.DeviceIdType.LOGICAL
F32 = jnp.float32
BF16 = jnp.bfloat16


def offset_parts(offset):
    return offset // 32, (offset // 8) % 4, (offset // 2) % 4, offset % 2


def hops(offset):
    z, x, y, c = offset_parts(offset)
    return 2 * (min(z, 4 - z) + min(x, 4 - x) + min(y, 4 - y)) + c


OFFSETS = sorted(range(1, NDEV), key=lambda o: -hops(o))


def peers():
    z, x, y, c = [lax.axis_index(a) for a in AXES]
    pz = [lax.rem(z + d, 4) * 32 for d in range(4)]
    px = [lax.rem(x + d, 4) * 8 for d in range(4)]
    py = [lax.rem(y + d, 4) * 2 for d in range(4)]
    pc = [lax.rem(c + d, 2) for d in range(2)]
    zx = [[pz[a] + px[b] for b in range(4)] for a in range(4)]
    yc = [[py[a] + pc[b] for b in range(2)] for a in range(4)]

    def index(offset):
        dz, dx, dy, dc = offset_parts(offset)
        return zx[dz][dx] + yc[dy][dc]

    return index


def halves(value):
    high = value.astype(BF16)
    low = (value - high.astype(F32)).astype(BF16)
    return high, low


def dot(a, b):
    return jnp.dot(a, b, preferred_element_type=F32)


def joined(pair):
    return pair[:, :PLANS] + pair[:, PLANS:]


def kernel(
    tile_ids,
    importance,
    influence,
    weights,
    tiles,
    owners,
    slots,
    structure,
    prescribed,
    step,
    new_weights,
    dose_out,
    staged,
    mat_hi,
    mat_lo,
    tra_hi,
    tra_lo,
    tile_buf,
    warp,
    warp_t,
    info_out,
    info_in,
    gather_in,
    gather_t,
    w_buf,
    w_cat,
    w_own,
    w_next,
    out_buf,
    in_buf,
    in_cat,
    dose,
    target_dose,
    voxel_weight,
    adj_cat,
    back_buf,
    adj_buf,
    la_cat,
    grad,
    grad_in,
    field_out,
    field_in,
    load_sem,
    tile_sem,
    info_ss,
    info_rs,
    w_ss,
    w_rs,
    out_ss,
    out_rs,
    back_ss,
    back_rs,
    grad_ss,
    grad_rs,
    field_ss,
    field_rs,
):
    index = peers()
    me = index(0)
    vox_of = lambda device: lax.rem(device, NVOX)

    def send_all(src, dst, send_sem, recv_sem):
        for o in OFFSETS:
            to = index(o)
            pltpu.make_async_remote_copy(
                src_ref=src(to),
                dst_ref=dst,
                send_sem=send_sem,
                recv_sem=recv_sem,
                device_id=to,
                device_id_type=LOGICAL,
            ).start()
        pltpu.make_async_copy(src(me), dst, recv_sem).start()

    def wait(ref, sem):
        pltpu.make_async_copy(ref, ref, sem).wait()

    loads = []
    for n in range(ROWS // LOAD):
        loads.append(
            pltpu.make_async_copy(
                influence.at[0, pl.ds(n * LOAD, LOAD)], staged.at[n % 4], load_sem.at[n % 4]
            )
        )
    for n in range(4):
        loads[n].start()
    tile_load = pltpu.make_async_copy(tiles, tile_buf, tile_sem)
    tile_load.start()

    barrier = pltpu.get_barrier_semaphore()
    for o in OFFSETS:
        pl.semaphore_signal(barrier, inc=1, device_id=index(o), device_id_type=LOGICAL)

    info_out[...] = jnp.zeros((BLK, BLK), F32)
    info_out[BLOCKS : 2 * BLOCKS, :] = structure[...].astype(F32)
    turned = info_out[...].T
    w_next[0:1, 0:BLOCKS] = (slots[...] * NVOX + owners[...]).astype(F32)
    lane = lax.broadcasted_iota(jnp.int32, (BLK, BLK), 1)
    info_out[...] = jnp.where(lane < BLOCKS, w_next[0:1, :], turned)

    for n in range(ROWS // LOAD):
        loads[n].wait()

        @pl.loop(0, SPOTS // BLK)
        def _(k, n=n):
            cols = pl.ds(pl.multiple_of(k * BLK, BLK), BLK)
            for h in range(LOAD // BLK):
                part = staged[n % 4, h * BLK : (h + 1) * BLK, cols]
                rows = pl.ds(n * LOAD + h * BLK, BLK)
                high, low = halves(part)
                mat_hi[rows, cols] = high
                mat_lo[rows, cols] = low
                high, low = halves(part.T)
                tra_hi[cols, rows] = high
                tra_lo[cols, rows] = low

        if n + 4 < ROWS // LOAD:
            loads[n + 4].start()

    tile_load.wait()

    @pl.loop(0, BLOCKS)
    def _(b):
        tile = tile_buf[tile_ids[0, b]]
        high, low = halves(tile)
        warp[b, :, 0:BLK] = high
        warp[b, :, BLK : 2 * BLK] = low
        warp[b, :, 2 * BLK :] = high
        high, low = halves(tile.T)
        warp_t[b, :, 0:BLK] = high
        warp_t[b, :, BLK : 2 * BLK] = low
        warp_t[b, :, 2 * BLK :] = high

    w_own[...] = weights[...]
    pl.semaphore_wait(barrier, NDEV - 1)
    send_all(lambda to: weights, w_buf.at[0, pl.ds(me * OWN, OWN)], w_ss.at[0], w_rs.at[0])
    send_all(
        lambda to: info_out.at[pl.ds(to, 1)], info_in.at[pl.ds(me, 1)], info_ss, info_rs
    )

    def warped(matrix, value):
        high, low = halves(value)
        return dot(matrix, jnp.concatenate([high, high, low], axis=0))

    def tables():
        wait(info_in, info_rs)
        info = info_in[...]
        turned = info.T
        down = lax.broadcasted_iota(jnp.int32, (TARGETS, BLK), 0).astype(F32)
        across = lax.broadcasted_iota(jnp.int32, (BLK, TARGETS), 1).astype(F32)
        for b in range(BLOCKS):
            at = slice(b * BLK, (b + 1) * BLK)
            gather_in[:, at] = jnp.where(down == turned[b : b + 1, :], 1.0, 0.0).astype(BF16)
            gather_t[at, :] = jnp.where(across == info[:, b : b + 1], 1.0, 0.0).astype(BF16)
            kind = info[0:NVOX, BLOCKS + b : BLOCKS + b + 1]
            goal = jnp.zeros((NVOX, PLANS), F32)
            scale = jnp.zeros((NVOX, PLANS), F32)
            for s in range(NSTRUCT):
                goal = jnp.where(kind == float(s), prescribed[s : s + 1, :], goal)
                scale = jnp.where(kind == float(s), importance[0, s], scale)
            target_dose[b * NVOX : (b + 1) * NVOX, :] = goal
            voxel_weight[b * NVOX : (b + 1) * NVOX, :] = scale

    @pl.loop(0, ITERS)
    def _(it):
        wait(w_buf.at[it], w_rs.at[it])
        high, low = halves(w_buf[it])
        w_cat[:, :PLANS] = high
        w_cat[:, PLANS:] = low
        for c in range(CHUNKS):

            @pl.loop(0, PER * BLK // GROUP)
            def _(g, c=c):
                rows = pl.ds(pl.multiple_of(c * PER * BLK + g * GROUP, GROUP), GROUP)
                part = joined(dot(mat_hi[rows, :], w_cat[...]))
                part = part + dot(mat_lo[rows, :], w_cat[:, :PLANS])
                for k in range(GROUP // BLK):
                    b = g * (GROUP // BLK) + k
                    out_buf[c, pl.ds(b, NDEV, stride=PER), :] = warped(
                        warp[c * PER + b], part[k * BLK : (k + 1) * BLK]
                    )

            send_all(
                lambda to, c=c: out_buf.at[c, pl.ds(to * PER, PER)],
                in_buf.at[it, c, pl.ds(me * PER, PER)],
                out_ss.at[c],
                out_rs.at[it, c],
            )

        @pl.when(it == 0)
        def _():
            tables()

        for c in range(CHUNKS):
            wait(in_buf.at[it, c], out_rs.at[it, c])
            for b in range(PER):
                high, low = halves(in_buf[it, c, pl.ds(b, NDEV, stride=PER), :])
                rows = slice((c * PER + b) * NDEV, (c * PER + b + 1) * NDEV)
                in_cat[rows, :PLANS] = high
                in_cat[rows, PLANS:] = low
            half = slice(c * PER * NDEV, (c + 1) * PER * NDEV)
            part = joined(dot(gather_in[:, half], in_cat[half, :]))
            dose[...] = part if c == 0 else dose[...] + part
        adjoint = voxel_weight[...] * (dose[...] - target_dose[...])
        high, low = halves(adjoint)
        adj_cat[:, :PLANS] = high
        adj_cat[:, PLANS:] = low
        for c in range(CHUNKS):
            for b in range(PER):
                rows = slice((c * PER + b) * NDEV, (c * PER + b + 1) * NDEV)
                back_buf[c, pl.ds(b, NDEV, stride=PER), :] = joined(
                    dot(gather_t[rows, :], adj_cat[...])
                )
            send_all(
                lambda to, c=c: back_buf.at[c, pl.ds(to * PER, PER)],
                adj_buf.at[it, c, pl.ds(me * PER, PER)],
                back_ss.at[c],
                back_rs.at[it, c],
            )

        @pl.when(it == ITERS - 1)
        def _():
            for b in range(BLOCKS):
                field_out[pl.ds(b, NVOX, stride=BLOCKS), :] = dose[b * NVOX : (b + 1) * NVOX, :]
            send_all(
                lambda to: field_out.at[pl.ds(vox_of(to) * BLOCKS, BLOCKS)],
                field_in.at[pl.ds(me * BLOCKS, BLOCKS)],
                field_ss,
                field_rs,
            )

        for c in range(CHUNKS):
            wait(out_buf.at[c, pl.ds(0, (NDEV - 1) * PER)], out_ss.at[c])
        for c in range(CHUNKS):
            wait(adj_buf.at[it, c], back_rs.at[it, c])
            for b in range(PER):
                value = warped(warp_t[c * PER + b], adj_buf[it, c, pl.ds(b, NDEV, stride=PER), :])
                high, low = halves(value)
                rows = slice((c * PER + b) * NDEV, (c * PER + b + 1) * NDEV)
                la_cat[rows, :PLANS] = high
                la_cat[rows, PLANS:] = low

        @pl.loop(0, SPOTS // GROUP)
        def _(g):
            rows = pl.ds(pl.multiple_of(g * GROUP, GROUP), GROUP)
            part = joined(dot(tra_hi[rows, :], la_cat[...]))
            grad[rows, :] = part + dot(tra_lo[rows, :], la_cat[:, :PLANS])

        send_all(
            lambda to: grad.at[pl.ds(to * OWN, OWN)],
            grad_in.at[it, pl.ds(me * OWN, OWN)],
            grad_ss,
            grad_rs.at[it],
        )
        for c in range(CHUNKS):
            wait(back_buf.at[c, pl.ds(0, (NDEV - 1) * PER)], back_ss.at[c])
        wait(grad_in.at[it], grad_rs.at[it])
        for r in range(OWN):
            total = jnp.sum(grad_in[it, pl.ds(r, NDEV, stride=OWN), :], axis=0, keepdims=True)
            w_next[r : r + 1, :] = jnp.maximum(w_own[r : r + 1, :] - step[...] * total, 0.0)
        w_own[...] = w_next[0:OWN, :]

        @pl.when(it < ITERS - 1)
        def _():
            send_all(
                lambda to: w_next.at[pl.ds(0, OWN)],
                w_buf.at[it + 1, pl.ds(me * OWN, OWN)],
                w_ss.at[it + 1],
                w_rs.at[it + 1],
            )
            wait(w_buf.at[it, pl.ds(0, (NDEV - 1) * OWN)], w_ss.at[it + 1])

        wait(grad.at[pl.ds(0, (NDEV - 1) * OWN)], grad_ss)

    new_weights[...] = w_own[...]
    wait(w_buf.at[0, pl.ds(0, (NDEV - 1) * OWN)], w_ss.at[0])
    wait(info_in.at[pl.ds(0, NDEV - 1)], info_ss)
    wait(field_in, field_rs)
    for b in range(BLOCKS):
        dose_out[b * BLK : (b + 1) * BLK, :] = field_in[pl.ds(b, NDEV, stride=BLOCKS), :]
    wait(field_in.at[pl.ds(0, (NDEV - 1) * BLOCKS)], field_ss)


def per_device(
    influence,
    weights,
    warp_tiles,
    owners,
    owner_slot,
    tile_index,
    structure,
    prescribed,
    importance,
    step_size,
):
    vmem = pl.BlockSpec(memory_space=pltpu.VMEM)
    smem = pl.BlockSpec(memory_space=pltpu.SMEM)
    hbm = pl.BlockSpec(memory_space=pl.ANY)
    dma = pltpu.SemaphoreType.DMA
    scratch = [
        pltpu.VMEM((4, LOAD, SPOTS), F32),
        pltpu.VMEM((ROWS, SPOTS), BF16),
        pltpu.VMEM((ROWS, SPOTS), BF16),
        pltpu.VMEM((SPOTS, ROWS), BF16),
        pltpu.VMEM((SPOTS, ROWS), BF16),
        pltpu.VMEM((NTILE, BLK, BLK), F32),
        pltpu.VMEM((BLOCKS, BLK, 3 * BLK), BF16),
        pltpu.VMEM((BLOCKS, BLK, 3 * BLK), BF16),
        pltpu.VMEM((BLK, BLK), F32),
        pltpu.VMEM((BLK, BLK), F32),
        pltpu.VMEM((TARGETS, SOURCES), BF16),
        pltpu.VMEM((SOURCES, TARGETS), BF16),
        pltpu.VMEM((ITERS, SPOTS, PLANS), F32),
        pltpu.VMEM((SPOTS, 2 * PLANS), BF16),
        pltpu.VMEM((OWN, PLANS), F32),
        pltpu.VMEM((16, PLANS), F32),
        pltpu.VMEM((CHUNKS, NDEV * PER, PLANS), F32),
        pltpu.VMEM((ITERS, CHUNKS, NDEV * PER, PLANS), F32),
        pltpu.VMEM((SOURCES, 2 * PLANS), BF16),
        pltpu.VMEM((TARGETS, PLANS), F32),
        pltpu.VMEM((TARGETS, PLANS), F32),
        pltpu.VMEM((TARGETS, PLANS), F32),
        pltpu.VMEM((TARGETS, 2 * PLANS), BF16),
        pltpu.VMEM((CHUNKS, NDEV * PER, PLANS), F32),
        pltpu.VMEM((ITERS, CHUNKS, NDEV * PER, PLANS), F32),
        pltpu.VMEM((ROWS, 2 * PLANS), BF16),
        pltpu.VMEM((SPOTS, PLANS), F32),
        pltpu.VMEM((ITERS, SPOTS, PLANS), F32),
        pltpu.VMEM((NVOX * BLOCKS, PLANS), F32),
        pltpu.VMEM((NDEV * BLOCKS, PLANS), F32),
        dma((4,)),
        dma,
        dma,
        dma,
        dma((ITERS,)),
        dma((ITERS,)),
        dma((CHUNKS,)),
        dma((ITERS, CHUNKS)),
        dma((CHUNKS,)),
        dma((ITERS, CHUNKS)),
        dma,
        dma((ITERS,)),
        dma,
        dma,
    ]
    return pl.pallas_call(
        kernel,
        out_shape=(
            jax.ShapeDtypeStruct((OWN, PLANS), F32),
            jax.ShapeDtypeStruct((ROWS, PLANS), F32),
        ),
        in_specs=[smem, smem, hbm, vmem, hbm, vmem, vmem, vmem, vmem, vmem],
        out_specs=(vmem, vmem),
        scratch_shapes=scratch,
        compiler_params=pltpu.CompilerParams(
            collective_id=0, has_side_effects=True, vmem_limit_bytes=67043328
        ),
    )(
        tile_index,
        importance.reshape(1, NSTRUCT),
        influence,
        weights,
        warp_tiles,
        owners.reshape(1, BLOCKS),
        owner_slot,
        structure.reshape(BLOCKS, BLK),
        prescribed,
        step_size.reshape(1, PLANS),
    )


def solution(mesh):
    split = Mesh(mesh.devices.reshape(SIZES), AXES)
    both = P("z", VOX)
    placed = (
        P("z", VOX, None),
        P(AXES, None),
        P(),
        P("z", VOX, None),
        both,
        both,
        P(VOX),
        P(),
        P(),
        P(),
    )
    return jax.shard_map(
        per_device,
        mesh=split,
        in_specs=placed,
        out_specs=(P(AXES, None), P(VOX, None)),
        check_vma=False,
    )
```

time: 592 us -> 154 us (0.26); the launches traced: 584 us -> 152 us
  blocking collectives: 292 us -> 0 us
  Pallas kernels: 0 us -> 148 us
  waiting for transfers between devices: 104 us -> 0 us
  matrix products: 85.8 us -> 0 us
  local copies, waits for them, and re-layouts: 59.5 us -> 3.56 us
  starting transfers between devices: 28.9 us -> 0 us
  other arithmetic: 13.2 us -> 0 us
    all_to_all x11 -> x0, blocking collectives: 292 us -> none  [the longest x2 114 us: per_device(): lax.all_to_all(back_slots.reshape(vox_count, CAP, block_rows * plans), VO...]
    pallas_call x0 -> x1, Pallas kernels: none -> 148 us  [per_device(): pl.pallas_call(kernel, out_shape=(jax.ShapeDtypeStruct((OWN, PLANS), F32)...]
    all_to_all x4 -> x0, waiting for transfers between devices: 104 us -> none  [the longest x2 52.8 us: copy_for_each(): return lax.all_to_all(copies, axis, split_axis=0, concat_axis=0, tiled=True)]
    dot_general x18 -> x0, matrix products: 85.8 us -> none  [the longest x2 29.5 us: per_device(): jnp.dot(matrix, gathered_by_axis(new_weights, (('phase', 'vox_0', 'vox_1'...]
    all_to_all x4 -> x0, starting transfers between devices: 28.9 us -> none  [the longest x2 17.5 us: copy_for_each(): return lax.all_to_all(copies, axis, split_axis=0, concat_axis=0, tiled=True)]
    reshape x9 -> x0, local copies, waits for them, and re-layouts: 17.7 us -> none  [the longest x2 12.1 us: per_device(): returned.reshape(slots_all, block_rows * plans)]
    dot_general x6 -> x0, local copies, waits for them, and re-layouts: 16.3 us -> none  [the longest x2 8.44 us: per_device(): jnp.dot(selector, warped.reshape(local_blocks, block_rows * plans), preci...]
    another operation x6 -> x0, local copies, waits for them, and re-layouts: 14.4 us -> none  [the longest x2 12.1 us: per_device(): warped_in.reshape(slots_all, block_rows * plans)]
  transfers between devices with their start and end apart: 4 -> 0, of which waited for: 3 -> 0; matrix products, arithmetic and copies ran while one was open for 5% -> 0% of each run, Pallas kernels for 0% -> 0%
where the time goes in v1:
time: 154 us; the launch traced here: 152 us
  Pallas kernels  148 us (96%)
  local copies, waits for them, and re-layouts  3.56 us (2%)
    pallas_call x1, Pallas kernels, per_device(): pl.pallas_call(kernel, out_shape=(jax.ShapeDtypeStruct((OWN, PLANS), F32)...  148 us
    unnamed x2, local copies, waits for them, and re-layouts  3.56 us

profile of v1, /device:TPU:1, one launch (start us, length us, event | category | flops | bytes accessed | tf_op | source)
XLA Modules:
  0.0 152.3 jit_solution(11536766818411040627)
XLA Ops:
  0.6 148.1 %shard_map.113 = (f32[12,128]{1,0:T(8,128)}, f32[2048,128]{1,0:T(8,128)}) custom-call(s32[1,16]{1,0:T(1,128)} %tile_ids.1, f32[1,8]{1,0:T(1,128)} %bitcast.5, f32[1,2048,1536]{2,1,0:T(8,128)} %influence.1, f32[12,128]{1,0:T(8,128)} %weights.1, f32[64,128,128]{2,1,0:T(8,128)} %tiles.1, s32[1,16]{1,0:T(1,128)} %bitcast.6, s32[1,16]{1,0:T(1,128)} %slots.1, ...), custom_call_target="tpu_custom_call" | custom-call | tf_op jit(solution)/shard_map/pallas_call | solution.py:422
  148.7 1.3 copy.14
  150.0 2.3 %copy.15 = f32[2048,128]{1,0:T(8,128)} copy(f32[2048,128]{1,0:T(8,128)} %get-tuple-element.5) | data formatting | bytes 2097152

commit v2 on v1

--- a/solution.py
+++ b/solution.py
@@ -26,6 +26,7 @@
 NTILE = 64
 LOAD = 256
 GROUP = 512
+LAYER = SPOTS // 4
 LOGICAL = pl.DeviceIdType.LOGICAL
 F32 = jnp.float32
 BF16 = jnp.bfloat16
@@ -135,22 +136,25 @@
     me = index(0)
     vox_of = lambda device: lax.rem(device, NVOX)
 
+    def send(src, dst, send_sem, recv_sem, to):
+        pltpu.make_async_remote_copy(
+            src_ref=src,
+            dst_ref=dst,
+            send_sem=send_sem,
+            recv_sem=recv_sem,
+            device_id=to,
+            device_id_type=LOGICAL,
+        ).start()
+
     def send_all(src, dst, send_sem, recv_sem):
         for o in OFFSETS:
-            to = index(o)
-            pltpu.make_async_remote_copy(
-                src_ref=src(to),
-                dst_ref=dst,
-                send_sem=send_sem,
-                recv_sem=recv_sem,
-                device_id=to,
-                device_id_type=LOGICAL,
-            ).start()
+            send(src(index(o)), dst, send_sem, recv_sem, index(o))
         pltpu.make_async_copy(src(me), dst, recv_sem).start()
 
     def wait(ref, sem):
         pltpu.make_async_copy(ref, ref, sem).wait()
 
+    stored = pltpu.make_async_copy(field_in, dose_out, tile_sem)
     loads = []
     for n in range(ROWS // LOAD):
         loads.append(
@@ -180,15 +184,10 @@
         @pl.loop(0, SPOTS // BLK)
         def _(k, n=n):
             cols = pl.ds(pl.multiple_of(k * BLK, BLK), BLK)
-            for h in range(LOAD // BLK):
-                part = staged[n % 4, h * BLK : (h + 1) * BLK, cols]
-                rows = pl.ds(n * LOAD + h * BLK, BLK)
-                high, low = halves(part)
-                mat_hi[rows, cols] = high
-                mat_lo[rows, cols] = low
-                high, low = halves(part.T)
-                tra_hi[cols, rows] = high
-                tra_lo[cols, rows] = low
+            rows = pl.ds(n * LOAD, LOAD)
+            high, low = halves(staged[n % 4, :, cols])
+            mat_hi[rows, cols] = high
+            mat_lo[rows, cols] = low
 
         if n + 4 < ROWS // LOAD:
             loads[n + 4].start()
@@ -213,6 +212,14 @@
     send_all(
         lambda to: info_out.at[pl.ds(to, 1)], info_in.at[pl.ds(me, 1)], info_ss, info_rs
     )
+
+    @pl.loop(0, SPOTS // BLK)
+    def _(k):
+        cols = pl.ds(pl.multiple_of(k * BLK, BLK), BLK)
+        for n in range(ROWS // GROUP):
+            rows = slice(n * GROUP, (n + 1) * GROUP)
+            tra_hi[cols, rows] = mat_hi[rows, cols].T
+            tra_lo[cols, rows] = mat_lo[rows, cols].T
 
     def warped(matrix, value):
         high, low = halves(value)
@@ -307,7 +314,7 @@
 
         for c in range(CHUNKS):
             wait(out_buf.at[c, pl.ds(0, (NDEV - 1) * PER)], out_ss.at[c])
-        for c in range(CHUNKS):
+        def spread(c):
             wait(adj_buf.at[it, c], back_rs.at[it, c])
             for b in range(PER):
                 value = warped(warp_t[c * PER + b], adj_buf[it, c, pl.ds(b, NDEV, stride=PER), :])
@@ -316,20 +323,36 @@
                 la_cat[rows, :PLANS] = high
                 la_cat[rows, PLANS:] = low
 
-        @pl.loop(0, SPOTS // GROUP)
+        def pulled(rows, c):
+            half = slice(c * PER * NDEV, (c + 1) * PER * NDEV)
+            part = joined(dot(tra_hi[rows, half], la_cat[half, :]))
+            return part + dot(tra_lo[rows, half], la_cat[half, :PLANS])
+
+        spread(0)
+
+        @pl.loop(0, SPOTS // LAYER)
         def _(g):
-            rows = pl.ds(pl.multiple_of(g * GROUP, GROUP), GROUP)
-            part = joined(dot(tra_hi[rows, :], la_cat[...]))
-            grad[rows, :] = part + dot(tra_lo[rows, :], la_cat[:, :PLANS])
-
-        send_all(
-            lambda to: grad.at[pl.ds(to * OWN, OWN)],
-            grad_in.at[it, pl.ds(me * OWN, OWN)],
-            grad_ss,
-            grad_rs.at[it],
-        )
+            rows = pl.ds(pl.multiple_of(g * LAYER, LAYER), LAYER)
+            grad[rows, :] = pulled(rows, 0)
+
+        spread(1)
+        own = grad_in.at[it, pl.ds(me * OWN, OWN)]
+        for dz in (2, 1, 3, 0):
+            first = index(dz * 32) // 32 * LAYER
+            rows = pl.ds(pl.multiple_of(first, LAYER), LAYER)
+            grad[rows, :] = grad[rows, :] + pulled(rows, 1)
+            for o in OFFSETS:
+                if o // 32 == dz:
+                    send(grad.at[pl.ds(index(o) * OWN, OWN)], own, grad_ss, grad_rs.at[it], index(o))
+        pltpu.make_async_copy(grad.at[pl.ds(me * OWN, OWN)], own, grad_rs.at[it]).start()
         for c in range(CHUNKS):
             wait(back_buf.at[c, pl.ds(0, (NDEV - 1) * PER)], back_ss.at[c])
+
+        @pl.when(it == ITERS - 1)
+        def _():
+            wait(field_in, field_rs)
+            stored.start()
+
         wait(grad_in.at[it], grad_rs.at[it])
         for r in range(OWN):
             total = jnp.sum(grad_in[it, pl.ds(r, NDEV, stride=OWN), :], axis=0, keepdims=True)
@@ -351,10 +374,14 @@
     new_weights[...] = w_own[...]
     wait(w_buf.at[0, pl.ds(0, (NDEV - 1) * OWN)], w_ss.at[0])
     wait(info_in.at[pl.ds(0, NDEV - 1)], info_ss)
-    wait(field_in, field_rs)
+    wait(field_in.at[pl.ds(0, (NDEV - 1) * BLOCKS)], field_ss)
+    stored.wait()
+
+
+def finish(weights, field, new_weights, dose_field):
+    new_weights[...] = weights[...]
     for b in range(BLOCKS):
-        dose_out[b * BLK : (b + 1) * BLK, :] = field_in[pl.ds(b, NDEV, stride=BLOCKS), :]
-    wait(field_in.at[pl.ds(0, (NDEV - 1) * BLOCKS)], field_ss)
+        dose_field[b * BLK : (b + 1) * BLK, :] = field[pl.ds(b, NDEV, stride=BLOCKS), :]
 
 
 def per_device(
@@ -419,14 +446,15 @@
         dma,
         dma,
     ]
-    return pl.pallas_call(
+    outs = (
+        jax.ShapeDtypeStruct((OWN, PLANS), F32),
+        jax.ShapeDtypeStruct((ROWS, PLANS), F32),
+    )
+    final_weights, field = pl.pallas_call(
         kernel,
-        out_shape=(
-            jax.ShapeDtypeStruct((OWN, PLANS), F32),
-            jax.ShapeDtypeStruct((ROWS, PLANS), F32),
-        ),
+        out_shape=outs,
         in_specs=[smem, smem, hbm, vmem, hbm, vmem, vmem, vmem, vmem, vmem],
-        out_specs=(vmem, vmem),
+        out_specs=(vmem, hbm),
         scratch_shapes=scratch,
         compiler_params=pltpu.CompilerParams(
             collective_id=0, has_side_effects=True, vmem_limit_bytes=67043328
@@ -443,6 +471,9 @@
         prescribed,
         step_size.reshape(1, PLANS),
     )
+    return pl.pallas_call(
+        finish, out_shape=outs, in_specs=[vmem, vmem], out_specs=(vmem, vmem)
+    )(final_weights, field)
 
 
 def solution(mesh):

time: 154 us -> 142 us (0.922)
  Pallas kernels: 148 us -> 141 us
  local copies, waits for them, and re-layouts: 3.56 us -> 0 us
    pallas_call x1 -> x2, Pallas kernels: 148 us -> 141 us  [the longest x1 139 us: per_device(): pl.pallas_call(kernel, out_shape=outs, in_specs=[smem, smem, hbm, vmem, h...]
    unnamed x2 -> x0, local copies, waits for them, and re-layouts: 3.56 us -> none
where the time goes in v2:
time: 142 us
  Pallas kernels  141 us (99%)
    pallas_call x1, Pallas kernels, per_device(): pl.pallas_call(kernel, out_shape=outs, in_specs=[smem, smem, hbm, vmem, h...  139 us

profile of v2, /device:TPU:1, one launch (start us, length us, event | category | flops | bytes accessed | tf_op | source)
XLA Modules:
  0.0 141.7 jit_solution(7438340286485830518)
XLA Ops:
  0.6 138.6 %shard_map.113 = (f32[12,128]{1,0:T(8,128)}, f32[2048,128]{1,0:T(8,128)}) custom-call(s32[1,16]{1,0:T(1,128)} %tile_ids.1, f32[1,8]{1,0:T(1,128)} %bitcast.5, f32[1,2048,1536]{2,1,0:T(8,128)} %influence.1, f32[12,128]{1,0:T(8,128)} %weights.1, f32[64,128,128]{2,1,0:T(8,128)} %tiles.1, s32[1,16]{1,0:T(1,128)} %bitcast.6, s32[1,16]{1,0:T(1,128)} %slots.1, ...), custom_call_target="tpu_custom_call" | custom-call | tf_op jit(solution)/shard_map/pallas_call | solution.py:453
  139.2 2.6 %shard_map.114 = (f32[12,128]{1,0:T(8,128)}, f32[2048,128]{1,0:T(8,128)}) custom-call(f32[12,128]{1,0:T(8,128)} %get-tuple-element.4.weights, f32[2048,128]{1,0:T(8,128)} %get-tuple-element.5.field), custom_call_target="tpu_custom_call" | custom-call | tf_op jit(solution)/shard_map/pallas_call | solution.py:474

commit v3 on v2

v3 whole, which is shorter than its diff:
```python
import jax
import jax.numpy as jnp
from jax import lax
from jax.experimental import pallas as pl
from jax.experimental.pallas import tpu as pltpu
from jax.sharding import Mesh
from jax.sharding import PartitionSpec as P

AXES = ("z", "x", "y", "c")
VOX = ("x", "y", "c")
SIZES = (4, 4, 4, 2)
NDEV = 128
NVOX = 32
NSTRUCT = 8
ITERS = 2
PLANS = 128
BLK = 128
BLOCKS = 16
PARTS = 2
PER = BLOCKS // PARTS
SPOTS = 1536
OWN = SPOTS // NDEV
PACKED = OWN // PARTS
ROWS = BLOCKS * BLK
TARGETS = NVOX * BLOCKS
SOURCES = NDEV * BLOCKS
NTILE = 64
LOAD = 256
LOADS = ROWS // LOAD
GROUP = 512
DEPOSIT = 0
LATE = 2
EARLY = 3
PAIR = GROUP // 2
LAYER = SPOTS // 4
LOGICAL = pl.DeviceIdType.LOGICAL
F32 = jnp.float32
BF16 = jnp.bfloat16


def offset_parts(offset):
    return offset // 32, (offset // 8) % 4, (offset // 2) % 4, offset % 2


def hops(offset):
    z, x, y, c = offset_parts(offset)
    return 2 * (min(z, 4 - z) + min(x, 4 - x) + min(y, 4 - y)) + c


OFFSETS = sorted(range(1, NDEV), key=lambda o: -hops(o))
CHIPS = [o for o in OFFSETS if o % 2 == 0]
NCHIP = NDEV // 2


def peers():
    z, x, y, c = [lax.axis_index(a) for a in AXES]
    pz = [lax.rem(z + d, 4) * 32 for d in range(4)]
    px = [lax.rem(x + d, 4) * 8 for d in range(4)]
    py = [lax.rem(y + d, 4) * 2 for d in range(4)]
    pc = [lax.rem(c + d, 2) for d in range(2)]
    zx = [[pz[a] + px[b] for b in range(4)] for a in range(4)]
    yc = [[py[a] + pc[b] for b in range(2)] for a in range(4)]

    def index(offset):
        dz, dx, dy, dc = offset_parts(offset)
        return zx[dz][dx] + yc[dy][dc]

    return index


def halves(value):
    high = value.astype(BF16)
    low = (value - high.astype(F32)).astype(BF16)
    return high, low


def dot(a, b):
    return jnp.dot(a, b, preferred_element_type=F32)


def left(rows):
    return lax.broadcasted_iota(jnp.int32, (rows, PLANS), 1) < PLANS // 2


def swapped(value):
    return pltpu.roll(value, PLANS // 2, 1)


def joined(pair):
    return pair[:, :PLANS] + pair[:, PLANS:]


def kernel(
    tile_ids,
    importance,
    influence,
    weights,
    tiles,
    owners,
    slots,
    structure,
    prescribed,
    step,
    new_weights,
    dose_out,
    staged,
    mat_hi,
    mat_lo,
    tra_hi,
    tra_lo,
    tile_buf,
    warp,
    warp_t,
    info_out,
    info_in,
    gather_in,
    gather_t,
    w_buf,
    w_flat,
    w_cat,
    w_own,
    step_buf,
    out_buf,
    in_buf,
    in_cat,
    dose,
    target_dose,
    voxel_weight,
    adj_cat,
    back_buf,
    adj_buf,
    la_cat,
    flat,
    grad,
    pair_in,
    grad_sum,
    grad_in,
    field_out,
    field_in,
    field,
    load_sem,
    tile_sem,
    info_ss,
    info_rs,
    w_ss,
    w_rs,
    pass_ss,
    pass_rs,
    out_ss,
    out_rs,
    back_ss,
    back_rs,
    pair_ss,
    pair_rs,
    grad_ss,
    grad_rs,
    field_ss,
    field_rs,
):
    index = peers()
    me = index(0)
    partner = index(1)
    chip = me // 2
    vox_of = lambda device: lax.rem(device, NVOX)

    def send(src, dst, send_sem, recv_sem, to):
        pltpu.make_async_remote_copy(
            src_ref=src,
            dst_ref=dst,
            send_sem=send_sem,
            recv_sem=recv_sem,
            device_id=to,
            device_id_type=LOGICAL,
        ).start()

    def send_all(src, dst, send_sem, recv_sem):
        for o in OFFSETS:
            send(src(index(o)), dst, send_sem, recv_sem, index(o))
        pltpu.make_async_copy(src(me), dst, recv_sem).start()

    def wait(ref, sem):
        pltpu.make_async_copy(ref, ref, sem).wait()

    stored = pltpu.make_async_copy(field, dose_out, tile_sem)
    loads = []
    for n in range(LOADS):
        loads.append(
            pltpu.make_async_copy(
                influence.at[0, pl.ds(n * LOAD, LOAD)], staged.at[n % 4], load_sem.at[n % 4]
            )
        )
    for n in range(4):
        loads[n].start()
    tile_load = pltpu.make_async_copy(tiles, tile_buf, tile_sem)
    tile_load.start()

    barrier = pltpu.get_barrier_semaphore()
    for o in OFFSETS:
        pl.semaphore_signal(barrier, inc=1, device_id=index(o), device_id_type=LOGICAL)

    info_out[...] = jnp.zeros((BLK, BLK), F32)
    info_out[BLOCKS : 2 * BLOCKS, :] = structure[...].astype(F32)
    turned = info_out[...].T
    flat[0:1, 0:BLOCKS] = (slots[...] * NVOX + owners[...]).astype(F32)
    lane = lax.broadcasted_iota(jnp.int32, (BLK, BLK), 1)
    info_out[...] = jnp.where(lane < BLOCKS, flat[0:1, :], turned)

    def place(b):
        return 2 * (b % PER) + b // PER

    def convert(n):
        loads[n].wait()

        @pl.loop(0, SPOTS // BLK)
        def _(k):
            cols = pl.ds(pl.multiple_of(k * BLK, BLK), BLK)
            for h in range(LOAD // BLK):
                high, low = halves(staged[n % 4, h * BLK : (h + 1) * BLK, cols])
                rows = pl.ds(place(n * (LOAD // BLK) + h) * BLK, BLK)
                mat_hi[rows, cols] = high
                mat_lo[rows, cols] = low

        if n + 4 < LOADS:
            loads[n + 4].start()

    for n in range(EARLY):
        convert(n)

    even = weights[pl.ds(0, PACKED, stride=2), :]
    odd = weights[pl.ds(1, PACKED, stride=2), :]
    w_own[0, 0, 0:PACKED, :] = jnp.where(left(PACKED), even, swapped(odd))
    w_own[0, 1, 0:PACKED, :] = jnp.where(left(PACKED), swapped(even), odd)
    step_buf[0:1, :] = jnp.where(left(1), step[...], swapped(step[...]))
    step_buf[1:2, :] = jnp.where(left(1), swapped(step[...]), step[...])
    pl.semaphore_wait(barrier, NDEV - 1)

    def share(it, h):
        source = w_own.at[it, h, pl.ds(0, PACKED)]
        own = w_buf.at[it, h, pl.ds(me * PACKED, PACKED)]
        for o in CHIPS:
            send(source, own, w_ss.at[it, h], w_rs.at[it, h], index(o))
        pltpu.make_async_copy(source, own, w_rs.at[it, h]).start()

    def forward(it, h):
        wait(w_buf.at[it, h, pl.ds(0, NCHIP * PACKED)], w_rs.at[it, h])
        for k in range(NCHIP):
            rows = w_buf.at[it, h, pl.ds((2 * k + me % 2) * PACKED, PACKED)]
            send(rows, rows, pass_ss.at[it, h], pass_rs.at[it, h], partner)

    send_all(
        lambda to: info_out.at[pl.ds(to, 1)], info_in.at[pl.ds(me, 1)], info_ss, info_rs
    )
    share(0, 0)
    share(0, 1)
    for n in range(EARLY, LOADS):
        convert(n)
    tile_load.wait()

    @pl.loop(0, BLOCKS)
    def _(b):
        tile = tile_buf[tile_ids[0, b]]
        high, low = halves(tile)
        warp[b, :, 0:BLK] = high
        warp[b, :, BLK : 2 * BLK] = low
        warp[b, :, 2 * BLK :] = high
        high, low = halves(tile.T)
        warp_t[b, :, 0:BLK] = high
        warp_t[b, :, BLK : 2 * BLK] = low
        warp_t[b, :, 2 * BLK :] = high

    def turn(h):
        @pl.loop(0, SPOTS // BLK // PARTS)
        def _(k):
            cols = pl.ds(pl.multiple_of(h * (SPOTS // PARTS) + k * BLK, BLK), BLK)
            for n in range(ROWS // GROUP):
                rows = slice(n * GROUP, (n + 1) * GROUP)
                tra_hi[cols, rows] = mat_hi[rows, cols].T
                tra_lo[cols, rows] = mat_lo[rows, cols].T

    def warped(matrix, value):
        high, low = halves(value)
        return dot(matrix, jnp.concatenate([high, high, low], axis=0))

    def tables():
        wait(info_in, info_rs)
        info = info_in[...]
        turned = info.T
        down = lax.broadcasted_iota(jnp.int32, (BLK, BLK), 0).astype(F32)
        across = lax.broadcasted_iota(jnp.int32, (1, BLK), 1).astype(F32)
        for b in range(BLOCKS):
            at = slice(b * BLK, (b + 1) * BLK)
            row, column = turned[b : b + 1, :], info[:, b : b + 1]
            for n in range(TARGETS // BLK):
                to = slice(n * BLK, (n + 1) * BLK)
                hit = down == row - float(n * BLK)
                gather_in[to, at] = jnp.where(hit, 1.0, 0.0).astype(BF16)
                hit = column == across + float(n * BLK)
                gather_t[at, to] = jnp.where(hit, 1.0, 0.0).astype(BF16)
            kind = info[0:NVOX, BLOCKS + b : BLOCKS + b + 1]
            goal = jnp.zeros((NVOX, PLANS), F32)
            scale = jnp.zeros((NVOX, PLANS), F32)
            for s in range(NSTRUCT):
                goal = jnp.where(kind == float(s), prescribed[s : s + 1, :], goal)
                scale = jnp.where(kind == float(s), importance[0, s], scale)
            at = slice(b * NVOX, (b + 1) * NVOX)
            target_dose[0, at, :] = jnp.where(left(NVOX), goal, swapped(goal))
            target_dose[1, at, :] = jnp.where(left(NVOX), swapped(goal), goal)
            voxel_weight[at, :] = scale

    forward(0, 0)
    tables()

    @pl.loop(0, ITERS)
    def _(it):
        @pl.loop(0, PARTS)
        def _(h):
            pl.when((it > 0) & (h == 0))(lambda: forward(it, h))
            wait(w_buf.at[it, h, pl.ds(0, NCHIP * PACKED)], pass_rs.at[it, h])
            pair = w_buf[it, h]
            turned = swapped(pair)
            near = left(SPOTS // 2)
            w_flat[pl.ds(0, SPOTS // 2, stride=2), :] = jnp.where(near, pair, turned)
            w_flat[pl.ds(1, SPOTS // 2, stride=2), :] = jnp.where(near, turned, pair)
            high, low = halves(w_flat[...])
            w_cat[:, :PLANS] = high
            w_cat[:, PLANS:] = low

            @pl.loop(0, ROWS // GROUP)
            def _(g):
                pl.when((g == LATE) & (h == 0))(lambda: forward(it, 1))
                rows = pl.ds(pl.multiple_of(g * GROUP, GROUP), GROUP)
                part = joined(dot(mat_hi[rows, :], w_cat[...]))
                part = part + dot(mat_lo[rows, :], w_cat[:, :PLANS])
                for k in range(PAIR // BLK):
                    b = g * (PAIR // BLK) + k
                    at = 2 * k * BLK
                    first = warped(warp[b], part[at : at + BLK])
                    second = warped(warp[PER + b], part[at + BLK : at + 2 * BLK])
                    out_buf[h, pl.ds(b, NDEV, stride=PER), :] = jnp.where(left(BLK), first, second)

            send_all(
                lambda to: out_buf.at[h, pl.ds(to * PER, PER)],
                in_buf.at[it, h, pl.ds(me * PER, PER)],
                out_ss.at[h],
                out_rs.at[it, h],
            )

        @pl.loop(0, PARTS)
        def _(h):
            pl.when(it == 0)(lambda: turn(h))
            wait(in_buf.at[it, h], out_rs.at[it, h])
            for b in range(PER):
                high, low = halves(in_buf[it, h, pl.ds(b, NDEV, stride=PER), :])
                in_cat[b * NDEV : (b + 1) * NDEV, :PLANS] = high
                in_cat[b * NDEV : (b + 1) * NDEV, PLANS:] = low
            near = left(TARGETS)
            total = jnp.where(
                near,
                joined(dot(gather_in[:, : PER * NDEV], in_cat[...])),
                joined(dot(gather_in[:, PER * NDEV :], in_cat[...])),
            )
            total = total + swapped(total)
            dose[h] = total
            high, low = halves(voxel_weight[...] * (total - target_dose[h]))
            adj_cat[:, :PLANS] = high
            adj_cat[:, PLANS:] = low
            for b in range(0, PER, PAIR // BLK):
                first = joined(dot(gather_t[b * NDEV : b * NDEV + PAIR, :], adj_cat[...]))
                second = (PER + b) * NDEV
                second = joined(dot(gather_t[second : second + PAIR, :], adj_cat[...]))
                both = jnp.where(left(PAIR), first, second)
                for k in range(PAIR // BLK):
                    back_buf[h, pl.ds(b + k, NDEV, stride=PER), :] = both[k * BLK : (k + 1) * BLK]
            send_all(
                lambda to: back_buf.at[h, pl.ds(to * PER, PER)],
                adj_buf.at[it, h, pl.ds(me * PER, PER)],
                back_ss.at[h],
                back_rs.at[it, h],
            )

        def deposit():
            for b in range(BLOCKS):
                rows = slice(b * NVOX, (b + 1) * NVOX)
                field_out[pl.ds(b, NVOX, stride=BLOCKS), :] = jnp.where(
                    left(NVOX), dose[0, rows, :], dose[1, rows, :]
                )
            send_all(
                lambda to: field_out.at[pl.ds(vox_of(to) * BLOCKS, BLOCKS)],
                field_in.at[pl.ds(me * BLOCKS, BLOCKS)],
                field_ss,
                field_rs,
            )

        @pl.loop(0, PARTS)
        def _(h):
            wait(adj_buf.at[it, h], back_rs.at[it, h])
            for b in range(PER):
                high, low = halves(adj_buf[it, h, pl.ds(b, NDEV, stride=PER), :])
                value = jnp.concatenate([high, high, low], axis=0)
                near = left(BLK)
                for block, here in ((b, near), (PER + b, ~near)):
                    high, low = halves(jnp.where(here, dot(warp_t[block], value), 0.0))
                    rows = slice(place(block) * BLK, (place(block) + 1) * BLK)
                    la_cat[rows, :PLANS] = high
                    la_cat[rows, PLANS:] = low
            own = grad_in.at[it, h, pl.ds(chip * PACKED, PACKED)]
            order = (2, 1, 3, 0)

            def deliver(n):
                first = index(order[n] * 32) // 32
                layer = pl.multiple_of(first * (LAYER // 2), LAYER // 2)
                rows = pl.ds(layer, LAYER // 2)
                wait(pair_in.at[it, h, pl.ds(0, LAYER // 4)], pair_rs.at[it, h, n])
                grad_sum[h, rows, :] = grad[h, rows, :] + pair_in[it, h, rows, :]
                for o in CHIPS:
                    if o // 32 == order[n]:
                        to = index(o)
                        source = grad_sum.at[h, pl.ds(to * PACKED, PACKED)]
                        send(source, own, grad_ss.at[h], grad_rs.at[it, h], to)

            for n, dz in enumerate(order):
                first = index(dz * 32) // 32
                rows = pl.ds(pl.multiple_of(first * LAYER, LAYER), LAYER)
                part = joined(dot(tra_hi[rows, :], la_cat[...]))
                part = part + dot(tra_lo[rows, :], la_cat[:, :PLANS])
                flat[...] = part + swapped(part)
                even = flat[pl.ds(0, LAYER // 2, stride=2), :]
                odd = flat[pl.ds(1, LAYER // 2, stride=2), :]
                rows = pl.ds(pl.multiple_of(first * (LAYER // 2), LAYER // 2), LAYER // 2)
                grad[h, rows, :] = jnp.where(left(LAYER // 2), even, odd)
                for k in range(NVOX // 2):
                    device = first * NVOX + 2 * k + partner % 2
                    rows = pl.ds(device * PACKED, PACKED)
                    send(
                        grad.at[h, rows],
                        pair_in.at[it, h, rows],
                        pair_ss.at[h],
                        pair_rs.at[it, h, n],
                        partner,
                    )
                if n > 0:
                    deliver(n - 1)
                if n == DEPOSIT:
                    pl.when((it == ITERS - 1) & (h == 0))(deposit)
            deliver(len(order) - 1)
            source = grad_sum.at[h, pl.ds(me * PACKED, PACKED)]
            pltpu.make_async_copy(source, own, grad_rs.at[it, h]).start()

        @pl.when(it == ITERS - 1)
        def _():
            wait(field_in, field_rs)
            for b in range(BLOCKS):
                field[b * BLK : (b + 1) * BLK, :] = field_in[pl.ds(b, NDEV, stride=BLOCKS), :]
            stored.start()

        @pl.loop(0, PARTS)
        def _(h):
            wait(grad_in.at[it, h], grad_rs.at[it, h])
            for r in range(PACKED):
                total = jnp.sum(
                    grad_in[it, h, pl.ds(r, NCHIP, stride=PACKED), :], axis=0, keepdims=True
                )
                w_own[it + 1, h, r : r + 1, :] = jnp.maximum(
                    w_own[it, h, r : r + 1, :] - step_buf[pl.ds(h, 1), :] * total, 0.0
                )

            @pl.when(it < ITERS - 1)
            def _():
                share(it + 1, h)

        @pl.loop(0, PARTS)
        def _(h):
            wait(out_buf.at[h, pl.ds(0, (NDEV - 1) * PER)], out_ss.at[h])
            wait(back_buf.at[h, pl.ds(0, (NDEV - 1) * PER)], back_ss.at[h])
            wait(grad.at[h, pl.ds(0, (NCHIP - 1) * PACKED)], grad_ss.at[h])
            wait(grad.at[h, pl.ds(0, NCHIP * PACKED)], pair_ss.at[h])
            wait(w_buf.at[0, h, pl.ds(0, (NCHIP - 1) * PACKED)], w_ss.at[it, h])
            wait(w_buf.at[0, h, pl.ds(0, NCHIP * PACKED)], pass_ss.at[it, h])

    first, second = w_own[ITERS, 0, 0:PACKED, :], w_own[ITERS, 1, 0:PACKED, :]
    even = jnp.where(left(PACKED), first, swapped(second))
    odd = jnp.where(left(PACKED), swapped(first), second)
    for r in range(PACKED):
        new_weights[2 * r : 2 * r + 1, :] = even[r : r + 1, :]
        new_weights[2 * r + 1 : 2 * r + 2, :] = odd[r : r + 1, :]
    wait(info_in.at[pl.ds(0, NDEV - 1)], info_ss)
    wait(field_in.at[pl.ds(0, (NDEV - 1) * BLOCKS)], field_ss)
    stored.wait()


def finish(weights, field, new_weights, dose_field, small, large, in_sem, out_sem):
    pairs = [(weights, small, new_weights)]
    for n in range(4):
        rows = pl.ds(n * (ROWS // 4), ROWS // 4)
        pairs.append((field.at[rows], large.at[rows], dose_field.at[rows]))
    reads = [pltpu.make_async_copy(a, b, in_sem.at[n]) for n, (a, b, _) in enumerate(pairs)]
    writes = [pltpu.make_async_copy(b, c, out_sem.at[n]) for n, (_, b, c) in enumerate(pairs)]
    for read in reads:
        read.start()
    for read, write in zip(reads, writes):
        read.wait()
        write.start()
    for write in writes:
        write.wait()


def per_device(
    influence,
    weights,
    warp_tiles,
    owners,
    owner_slot,
    tile_index,
    structure,
    prescribed,
    importance,
    step_size,
):
    vmem = pl.BlockSpec(memory_space=pltpu.VMEM)
    smem = pl.BlockSpec(memory_space=pltpu.SMEM)
    hbm = pl.BlockSpec(memory_space=pl.ANY)
    dma = pltpu.SemaphoreType.DMA
    scratch = [
        pltpu.VMEM((4, LOAD, SPOTS), F32),
        pltpu.VMEM((ROWS, SPOTS), BF16),
        pltpu.VMEM((ROWS, SPOTS), BF16),
        pltpu.VMEM((SPOTS, ROWS), BF16),
        pltpu.VMEM((SPOTS, ROWS), BF16),
        pltpu.VMEM((NTILE, BLK, BLK), F32),
        pltpu.VMEM((BLOCKS, BLK, 3 * BLK), BF16),
        pltpu.VMEM((BLOCKS, BLK, 3 * BLK), BF16),
        pltpu.VMEM((BLK, BLK), F32),
        pltpu.VMEM((BLK, BLK), F32),
        pltpu.VMEM((TARGETS, SOURCES), BF16),
        pltpu.VMEM((SOURCES, TARGETS), BF16),
        pltpu.VMEM((ITERS, PARTS, SPOTS // 2, PLANS), F32),
        pltpu.VMEM((SPOTS, PLANS), F32),
        pltpu.VMEM((SPOTS, 2 * PLANS), BF16),
        pltpu.VMEM((ITERS + 1, PARTS, 8, PLANS), F32),
        pltpu.VMEM((8, PLANS), F32),
        pltpu.VMEM((PARTS, NDEV * PER, PLANS), F32),
        pltpu.VMEM((ITERS, PARTS, NDEV * PER, PLANS), F32),
        pltpu.VMEM((NDEV * PER, 2 * PLANS), BF16),
        pltpu.VMEM((PARTS, TARGETS, PLANS), F32),
        pltpu.VMEM((PARTS, TARGETS, PLANS), F32),
        pltpu.VMEM((TARGETS, PLANS), F32),
        pltpu.VMEM((TARGETS, 2 * PLANS), BF16),
        pltpu.VMEM((PARTS, NDEV * PER, PLANS), F32),
        pltpu.VMEM((ITERS, PARTS, NDEV * PER, PLANS), F32),
        pltpu.VMEM((ROWS, 2 * PLANS), BF16),
        pltpu.VMEM((LAYER, PLANS), F32),
        pltpu.VMEM((PARTS, SPOTS // 2, PLANS), F32),
        pltpu.VMEM((ITERS, PARTS, SPOTS // 2, PLANS), F32),
        pltpu.VMEM((PARTS, SPOTS // 2, PLANS), F32),
        pltpu.VMEM((ITERS, PARTS, NCHIP * PACKED, PLANS), F32),
        pltpu.VMEM((NVOX * BLOCKS, PLANS), F32),
        pltpu.VMEM((NDEV * BLOCKS, PLANS), F32),
        pltpu.VMEM((ROWS, PLANS), F32),
        dma((4,)),
        dma,
        dma,
        dma,
        dma((ITERS, PARTS)),
        dma((ITERS, PARTS)),
        dma((ITERS, PARTS)),
        dma((ITERS, PARTS)),
        dma((PARTS,)),
        dma((ITERS, PARTS)),
        dma((PARTS,)),
        dma((ITERS, PARTS)),
        dma((PARTS,)),
        dma((ITERS, PARTS, 4)),
        dma((PARTS,)),
        dma((ITERS, PARTS)),
        dma,
        dma,
    ]
    outs = (
        jax.ShapeDtypeStruct((OWN, PLANS), F32),
        jax.ShapeDtypeStruct((ROWS, PLANS), F32),
    )
    final_weights, field = pl.pallas_call(
        kernel,
        out_shape=outs,
        in_specs=[smem, smem, hbm, vmem, hbm, vmem, vmem, vmem, vmem, vmem],
        out_specs=(vmem, hbm),
        scratch_shapes=scratch,
        compiler_params=pltpu.CompilerParams(
            collective_id=0, has_side_effects=True, vmem_limit_bytes=67043328
        ),
    )(
        tile_index,
        importance.reshape(1, NSTRUCT),
        influence,
        weights,
        warp_tiles,
        owners.reshape(1, BLOCKS),
        owner_slot,
        structure.reshape(BLOCKS, BLK),
        prescribed,
        step_size.reshape(1, PLANS),
    )
    return pl.pallas_call(
        finish,
        out_shape=outs,
        in_specs=[hbm, hbm],
        out_specs=(hbm, hbm),
        scratch_shapes=[
            pltpu.VMEM((OWN, PLANS), F32),
            pltpu.VMEM((ROWS, PLANS), F32),
            dma((5,)),
            dma((5,)),
        ],
    )(final_weights, field)


def solution(mesh):
    split = Mesh(mesh.devices.reshape(SIZES), AXES)
    both = P("z", VOX)
    placed = (
        P("z", VOX, None),
        P(AXES, None),
        P(),
        P("z", VOX, None),
        both,
        both,
        P(VOX),
        P(),
        P(),
        P(),
    )
    return jax.shard_map(
        per_device,
        mesh=split,
        in_specs=placed,
        out_specs=(P(AXES, None), P(VOX, None)),
        check_vma=False,
    )
```

time: 142 us -> 126 us (0.89)
  Pallas kernels: 141 us -> 125 us
    pallas_call x1, Pallas kernels: 139 us -> 123 us  [per_device(): pl.pallas_call(kernel, out_shape=outs, in_specs=[smem, smem, hbm, vmem, h...]
where the time goes in v3:
time: 126 us
  Pallas kernels  125 us (99%)
    pallas_call x1, Pallas kernels, per_device(): pl.pallas_call(kernel, out_shape=outs, in_specs=[smem, smem, hbm, vmem, h...  123 us

profile of v3, /device:TPU:1, one launch (start us, length us, event | category | flops | bytes accessed | tf_op | source)
XLA Modules:
  0.0 125.7 jit_solution(5639969860702531171)
XLA Ops:
  0.6 122.9 %shard_map.113 = (f32[12,128]{1,0:T(8,128)}, f32[2048,128]{1,0:T(8,128)}) custom-call(s32[1,16]{1,0:T(1,128)} %tile_ids.1, f32[1,8]{1,0:T(1,128)} %bitcast.5, f32[1,2048,1536]{2,1,0:T(8,128)} %influence.1, f32[12,128]{1,0:T(8,128)} %weights.1, f32[64,128,128]{2,1,0:T(8,128)} %tiles.1, s32[1,16]{1,0:T(1,128)} %bitcast.6, s32[1,16]{1,0:T(1,128)} %slots.1, ...), custom_call_target="tpu_custom_call" | custom-call | tf_op jit(solution)/shard_map/pallas_call | solution.py:582
  123.5 2.0 %shard_map.114 = (f32[12,128]{1,0:T(8,128)}, f32[2048,128]{1,0:T(8,128)}) custom-call(f32[12,128]{1,0:T(8,128)} %get-tuple-element.4.weights, f32[2048,128]{1,0:T(8,128)} %get-tuple-element.5.field), custom_call_target="tpu_custom_call" | custom-call | tf_op jit(solution)/shard_map/pallas_call | solution.py:603

commit v4 on v3

--- a/solution.py
+++ b/solution.py
@@ -30,6 +30,7 @@
 GROUP = 512
 DEPOSIT = 0
 LATE = 2
+PLANE = NVOX * BLOCKS
 EARLY = 3
 PAIR = GROUP // 2
 LAYER = SPOTS // 4
@@ -156,6 +157,8 @@
     grad_rs,
     field_ss,
     field_rs,
+    relay_ss,
+    relay_rs,
 ):
     index = peers()
     me = index(0)
@@ -384,12 +387,24 @@
                 field_out[pl.ds(b, NVOX, stride=BLOCKS), :] = jnp.where(
                     left(NVOX), dose[0, rows, :], dose[1, rows, :]
                 )
-            send_all(
-                lambda to: field_out.at[pl.ds(vox_of(to) * BLOCKS, BLOCKS)],
-                field_in.at[pl.ds(me * BLOCKS, BLOCKS)],
-                field_ss,
-                field_rs,
-            )
+            own = field_in.at[pl.ds(me * BLOCKS, BLOCKS)]
+            for o in OFFSETS:
+                if o // 32 != 2:
+                    source = field_out.at[pl.ds(vox_of(index(o)) * BLOCKS, BLOCKS)]
+                    send(source, own, field_ss, field_rs.at[o // 32], index(o))
+            source = field_out.at[pl.ds(vox_of(me) * BLOCKS, BLOCKS)]
+            pltpu.make_async_copy(source, own, field_rs.at[0]).start()
+
+        def plane(dz):
+            return pl.multiple_of(index(dz * 32) // 32 * PLANE, PLANE)
+
+        def relay():
+            wait(field_in.at[pl.ds(plane(3), PLANE)], field_rs.at[1])
+            rows = field_in.at[pl.ds(plane(3), PLANE // 2)]
+            send(rows, rows, relay_ss.at[0], relay_rs.at[0], index(32))
+            wait(field_in.at[pl.ds(plane(1), PLANE)], field_rs.at[3])
+            rows = field_in.at[pl.ds(plane(1) + PLANE // 2, PLANE // 2)]
+            send(rows, rows, relay_ss.at[1], relay_rs.at[1], index(96))
 
         @pl.loop(0, PARTS)
         def _(h):
@@ -448,7 +463,11 @@
 
         @pl.when(it == ITERS - 1)
         def _():
-            wait(field_in, field_rs)
+            relay()
+            wait(field_in.at[pl.ds(plane(0), PLANE)], field_rs.at[0])
+            for k in range(2):
+                half = field_in.at[pl.ds(plane(2) + k * (PLANE // 2), PLANE // 2)]
+                wait(half, relay_rs.at[k])
             for b in range(BLOCKS):
                 field[b * BLK : (b + 1) * BLK, :] = field_in[pl.ds(b, NDEV, stride=BLOCKS), :]
             stored.start()
@@ -484,7 +503,9 @@
         new_weights[2 * r : 2 * r + 1, :] = even[r : r + 1, :]
         new_weights[2 * r + 1 : 2 * r + 2, :] = odd[r : r + 1, :]
     wait(info_in.at[pl.ds(0, NDEV - 1)], info_ss)
-    wait(field_in.at[pl.ds(0, (NDEV - 1) * BLOCKS)], field_ss)
+    wait(field_in.at[pl.ds(0, 3 * PLANE - BLOCKS)], field_ss)
+    for k in range(2):
+        wait(field_in.at[pl.ds(0, PLANE // 2)], relay_ss.at[k])
     stored.wait()
 
 
@@ -573,7 +594,9 @@
         dma((PARTS,)),
         dma((ITERS, PARTS)),
         dma,
-        dma,
+        dma((4,)),
+        dma((2,)),
+        dma((2,)),
     ]
     outs = (
         jax.ShapeDtypeStruct((OWN, PLANS), F32),

time: 126 us -> 123 us (0.976)
  Pallas kernels: 125 us -> 122 us
    pallas_call x1, Pallas kernels: 123 us -> 120 us  [per_device(): pl.pallas_call(kernel, out_shape=outs, in_specs=[smem, smem, hbm, vmem, h...]
where the time goes in v4:
time: 123 us
  Pallas kernels  122 us (99%)
    pallas_call x1, Pallas kernels, per_device(): pl.pallas_call(kernel, out_shape=outs, in_specs=[smem, smem, hbm, vmem, h...  120 us

profile of v4, /device:TPU:1, one launch (start us, length us, event | category | flops | bytes accessed | tf_op | source)
XLA Modules:
  0.0 123.3 jit_solution(15566523934560476276)
XLA Ops:
  0.6 120.5 %shard_map.113 = (f32[12,128]{1,0:T(8,128)}, f32[2048,128]{1,0:T(8,128)}) custom-call(s32[1,16]{1,0:T(1,128)} %tile_ids.1, f32[1,8]{1,0:T(1,128)} %bitcast.5, f32[1,2048,1536]{2,1,0:T(8,128)} %influence.1, f32[12,128]{1,0:T(8,128)} %weights.1, f32[64,128,128]{2,1,0:T(8,128)} %tiles.1, s32[1,16]{1,0:T(1,128)} %bitcast.6, s32[1,16]{1,0:T(1,128)} %slots.1, ...), custom_call_target="tpu_custom_call" | custom-call | tf_op jit(solution)/shard_map/pallas_call | solution.py:605
  121.1 2.0 %shard_map.114 = (f32[12,128]{1,0:T(8,128)}, f32[2048,128]{1,0:T(8,128)}) custom-call(f32[12,128]{1,0:T(8,128)} %get-tuple-element.4.weights, f32[2048,128]{1,0:T(8,128)} %get-tuple-element.5.field), custom_call_target="tpu_custom_call" | custom-call | tf_op jit(solution)/shard_map/pallas_call | solution.py:626

commit v5 on v4

--- a/solution.py
+++ b/solution.py
@@ -457,13 +457,13 @@
                     deliver(n - 1)
                 if n == DEPOSIT:
                     pl.when((it == ITERS - 1) & (h == 0))(deposit)
+            pl.when((it == ITERS - 1) & (h == PARTS - 1))(relay)
             deliver(len(order) - 1)
             source = grad_sum.at[h, pl.ds(me * PACKED, PACKED)]
             pltpu.make_async_copy(source, own, grad_rs.at[it, h]).start()
 
         @pl.when(it == ITERS - 1)
         def _():
-            relay()
             wait(field_in.at[pl.ds(plane(0), PLANE)], field_rs.at[0])
             for k in range(2):
                 half = field_in.at[pl.ds(plane(2) + k * (PLANE // 2), PLANE // 2)]

time: 123 us -> 124 us (level)
  no operation moved by 1% of the time
where the time goes in v5:
time: 124 us
  Pallas kernels  123 us (99%)
    pallas_call x1, Pallas kernels, per_device(): pl.pallas_call(kernel, out_shape=outs, in_specs=[smem, smem, hbm, vmem, h...  121 us

profile of v5, /device:TPU:1, one launch (start us, length us, event | category | flops | bytes accessed | tf_op | source)
XLA Modules:
  0.0 123.6 jit_solution(8315620196269147647)
XLA Ops:
  0.6 120.8 %shard_map.113 = (f32[12,128]{1,0:T(8,128)}, f32[2048,128]{1,0:T(8,128)}) custom-call(s32[1,16]{1,0:T(1,128)} %tile_ids.1, f32[1,8]{1,0:T(1,128)} %bitcast.5, f32[1,2048,1536]{2,1,0:T(8,128)} %influence.1, f32[12,128]{1,0:T(8,128)} %weights.1, f32[64,128,128]{2,1,0:T(8,128)} %tiles.1, s32[1,16]{1,0:T(1,128)} %bitcast.6, s32[1,16]{1,0:T(1,128)} %slots.1, ...), custom_call_target="tpu_custom_call" | custom-call | tf_op jit(solution)/shard_map/pallas_call | solution.py:605
  121.4 2.0 %shard_map.114 = (f32[12,128]{1,0:T(8,128)}, f32[2048,128]{1,0:T(8,128)}) custom-call(f32[12,128]{1,0:T(8,128)} %get-tuple-element.4.weights, f32[2048,128]{1,0:T(8,128)} %get-tuple-element.5.field), custom_call_target="tpu_custom_call" | custom-call | tf_op jit(solution)/shard_map/pallas_call | solution.py:626
